TPU v7x, 512 devices: a whole 4x4x16 slice. The times are simulated.
512 devices in a mesh: dom: 32 (over x_lo, z), grid: 16 (over x_hi, y, core).
Axes of the slice: x: 4 (x_hi: 2, x_lo: 2; x = x_hi * 2 + x_lo), y: 4, z: 16, core: 2. Of those that a mesh axis runs over, the one named last changes fastest.
Arguments:
- node_feats: bfloat16 [65536, 512], P(('dom', 'grid')), may hold values from -6 to 6
- adj_vals: bfloat16 [32, 16, 16, 4, 128, 128], P('dom', 'grid'), may hold values from -0.109375 to 0.109375
- adj_col: int32 [32, 16, 16, 4], P('dom', 'grid'), may hold values from 0 to 31
- adj_count: int32 [32, 16, 16], P('dom', 'grid'), may hold values from 0 to 4, as said below
- hist_store: bfloat16 [512, 16384], P('grid', 'dom'), may hold values from -6 to 6
- hist_list: int32 [32, 40], replicated, may hold values from 0 to 127, as said below
- hist_adj: bfloat16 [32, 40, 128, 128], P('dom'), may hold values from -0.3125 to 0.3125
- hist_row: int32 [32, 40], P('dom'), may hold values from 0 to 15
- hist_col: int32 [32, 40], P('dom'), may hold values from 0 to 39, each once within a row
- w_first: bfloat16 [512, 512], replicated, may hold values from -0.25 to 0.25
- w_second: bfloat16 [512, 512], replicated, may hold values from -0.25 to 0.25
Outputs:
- hidden: bfloat16 [65536, 512], P(('dom', 'grid'))
- embedding: bfloat16 [65536, 512], P(('dom', 'grid'))
Inputs may be any that keep to these rules, and one draw needn't show every extreme that they name: `adj_count`: slots of a block row at or beyond its count hold values that take no part. Some block row of some tile has 4 live slots. `hist_list`: the ids in one partition's list are distinct; at most 2 of them belong to one owner partition (owner = id // 4), and some list has 2 from one owner.
All inputs are finite; a program needn't handle non-finite values.
Results may differ from a plain program's by a relative error of at most 0.024.
Values may be sent and summed in bfloat16 or wider, within the bound.
No kernel may reach another device: no remote copies, remote signals or barrier semaphores. Data moves between devices by JAX's collectives and lax.ppermute only.
A program may use at most 64 MiB of HBM per device.

v0:
```python
import jax
import jax.numpy as jnp
from jax import lax
from jax.sharding import PartitionSpec as P

F = 512
BLOCK = 128
HOWN = 4
CAP = 2


def tile_product(col_panel, live_vals, tile_cols):
    blocks = col_panel.reshape(-1, BLOCK, col_panel.shape[1])
    picked = jnp.take(blocks, tile_cols, axis=0)
    summed = jnp.einsum("rkab,rkbf->raf", live_vals, picked, preferred_element_type=jnp.float32)
    return summed.reshape(-1, col_panel.shape[1])


def aggregate(source, live_vals, tile_cols, extra_term):
    col_panel = lax.all_gather(source, "dom", axis=0, tiled=True)
    partial_value = tile_product(col_panel, live_vals, tile_cols)
    if extra_term is not None:
        partial_value = partial_value + extra_term
    rounded = lax.optimization_barrier(partial_value.astype(jnp.bfloat16))
    return lax.psum_scatter(
        rounded.astype(jnp.float32).astype(jnp.bfloat16), "grid", scatter_dimension=0, tiled=True
    )


def history_term(hist_store, hist_list, local_adj, local_rows, local_cols, tile_rows):
    list_length = hist_list.shape[1]
    dom_index = lax.axis_index("dom")
    owner_ids = hist_list // HOWN
    local_ids = hist_list % HOWN
    same_owner = owner_ids[:, :, None] == owner_ids[:, None, :]
    earlier = jnp.arange(list_length)[None, :] < jnp.arange(list_length)[:, None]
    order_rank = jnp.sum(same_owner & earlier[None, :, :], axis=2)
    chosen_mask = (owner_ids == dom_index)[:, :, None, None]
    chosen_mask = chosen_mask & (
        order_rank[:, :, None, None] == jnp.arange(CAP)[None, None, :, None]
    )
    chosen_mask = chosen_mask & (
        local_ids[:, :, None, None] == jnp.arange(HOWN)[None, None, None, :]
    )
    selector = jnp.sum(chosen_mask.astype(jnp.int32), axis=1).astype(jnp.bfloat16)
    own_blocks = hist_store.reshape(hist_store.shape[0], HOWN, BLOCK)
    outgoing = jnp.einsum(
        "rch,fhb->rcfb", selector, own_blocks, preferred_element_type=jnp.float32
    ).astype(jnp.bfloat16)
    incoming = lax.all_to_all(outgoing, "dom", split_axis=0, concat_axis=0, tiled=True)
    flat_blocks = incoming.reshape(-1, incoming.shape[2], incoming.shape[3])
    mine_owner = lax.dynamic_index_in_dim(owner_ids, dom_index, 0, keepdims=False)
    mine_rank = lax.dynamic_index_in_dim(order_rank, dom_index, 0, keepdims=False)
    fetched = jnp.take(flat_blocks, mine_owner * CAP + mine_rank, axis=0)
    chosen = jnp.take(fetched, local_cols, axis=0)
    contribs = jnp.einsum("sfb,sab->sfa", chosen, local_adj, preferred_element_type=jnp.float32)
    row_onehot = (local_rows[None, :] == jnp.arange(tile_rows)[:, None]).astype(jnp.float32)
    summed = jnp.einsum("rs,sfa->rfa", row_onehot, contribs, precision=lax.Precision.HIGHEST)
    return summed.transpose(0, 2, 1).reshape(tile_rows * BLOCK, -1)


def local(
    node_feats,
    adj_vals,
    adj_col,
    adj_count,
    hist_store,
    hist_list,
    hist_adj,
    hist_row,
    hist_col,
    w_first,
    w_second,
):
    tile_vals = adj_vals[0, 0]
    tile_cols = adj_col[0, 0]
    row_counts = adj_count[0, 0]
    tile_rows = tile_vals.shape[0]
    live_mask = (jnp.arange(tile_vals.shape[1])[None, :] < row_counts[:, None]).astype(jnp.bfloat16)
    live_vals = tile_vals * live_mask[:, :, None, None]
    agg_first = aggregate(node_feats, live_vals, tile_cols, None)
    hidden = jax.nn.relu(jnp.dot(agg_first, w_first, preferred_element_type=jnp.float32)).astype(
        jnp.bfloat16
    )
    hist_part = history_term(
        hist_store, hist_list, hist_adj[0], hist_row[0], hist_col[0], tile_rows
    )
    grid_index = lax.axis_index("grid")
    placed = lax.dynamic_update_slice_in_dim(
        jnp.zeros((hist_part.shape[0], F), jnp.float32),
        hist_part,
        grid_index * hist_part.shape[1],
        1,
    )
    agg_second = aggregate(hidden, live_vals, tile_cols, placed)
    embedding = jnp.dot(agg_second, w_second, preferred_element_type=jnp.float32).astype(
        jnp.bfloat16
    )
    return (hidden, embedding)


def solution(mesh):
    placed = (
        P(("dom", "grid"), None),
        P("dom", "grid", None, None, None, None),
        P("dom", "grid", None, None),
        P("dom", "grid", None),
        P("grid", "dom"),
        P(),
        P("dom", None, None, None),
        P("dom", None),
        P("dom", None),
        P(),
        P(),
    )
    return jax.shard_map(
        local,
        mesh=mesh,
        in_specs=placed,
        out_specs=(P(("dom", "grid"), None), P(("dom", "grid"), None)),
        check_vma=False,
    )
```

profile of v0, /device:TPU:32, one launch (start us, length us, event | category | flops | bytes accessed | tf_op | source)
XLA Modules:
  0.0 524.1 jit_solution(14827638974284658832)
XLA Ops:
  7.2 0.7 all-gather.3.cloned.1.call-update
  8.0 0.7 compare_select_fusion
  8.8 0.7 compare_and_fusion
  9.6 0.7 fusion.22
  10.3 141.5 %all-gather.3.cloned.1.call-done = bf16[4096,512]{1,0:T(8,128)(2,1)} async-done(((bf16[128,512]{1,0:T(8,128)(2,1)}), bf16[4096,512]{1,0:T(8,128)(2,1)}) %all-gather.3.cloned.1.call-update) | async-done | bytes 4194320 | tf_op jit(solution)/shard_map/all_gather | solution.py:20
  151.8 7.7 %gather_fusion.2 = bf16[64,128,512]{2,1,0:T(8,128)(2,1)} fusion(bf16[32,128,512]{2,1,0:T(8,128)(2,1)} %bitcast.56, s32[1024]{0:T(1024)S(1)} %pad_clamp_fusion.2), kind=kCustom, calls=%fused_computation.clone | custom fusion | bytes 16777472 | tf_op jit(solution)/shard_map/jit(_take)/gather | solution.py:14
  159.5 7.2 %bitcast_convert_fusion = bf16[16,128,512]{2,1,0:T(8,128)(2,1)} fusion(bf16[16,4,128,512]{3,2,1,0:T(8,128)(2,1)} %bitcast.58, pred[16,4]{1,0:T(8,128)(4,1)S(1)} %copy.31, bf16[1,1,16,4,128,128]{5,4,3,2,1,0:T(8,128)(2,1)} %param.14, bf16[16,4]{1,0:T(8,128)(2,1)S(1)} %fusion.22), kind=kOutput, calls=%fused_computation.10 | convolution fusion | flops 1080033280 | bytes 12583104 | tf_op jit(solution)/shard_map/rkab,rkbf->raf/dot_general | solution.py:15
  166.8 87.4 %reduce-scatter.3.cloned.1.call-done = bf16[128,512]{1,0:T(8,128)(2,1)} async-done(((bf16[2048,512]{1,0:T(8,128)(2,1)}), bf16[128,512]{1,0:T(8,128)(2,1)}) %reduce-scatter.3.cloned.1.call-update) | async-done | bytes 131088 | tf_op jit(solution)/shard_map/reduce_scatter | solution.py:25
  254.2 1.8 fusion.12
  256.2 0.8 convert_reduce_fusion
  257.6 1.0 copy.35
  258.6 13.0 %all-to-all-start = ((bf16[32,2,32,128]{3,2,1,0:T(8,128)(2,1)}), bf16[32,2,32,128]{3,2,1,0:T(8,128)(2,1)S(1)}, u32[]{:S(2)}, u32[]{:S(2)}) async-start(bf16[32,2,32,128]{3,2,1,0:T(8,128)(2,1)} %copy.35), calls=%async_computation.1 | async-start | bytes 1048576 | tf_op jit(solution)/shard_map/all_to_all | solution.py:50
  271.8 36.6 %all-to-all-done = bf16[32,2,32,128]{3,2,1,0:T(8,128)(2,1)S(1)} async-done(((bf16[32,2,32,128]{3,2,1,0:T(8,128)(2,1)}), bf16[32,2,32,128]{3,2,1,0:T(8,128)(2,1)S(1)}, u32[]{:S(2)}, u32[]{:S(2)}) %all-to-all-start) | async-done | bytes 524320 | tf_op jit(solution)/shard_map/all_to_all | solution.py:50
  309.2 0.6 gather_fusion.1
  309.8 0.8 fusion.10
  310.6 0.7 convolution_bitcast_fusion
  311.7 91.9 %all-gather.5.cloned.1.call-done = bf16[4096,512]{1,0:T(8,128)(2,1)} async-done(((bf16[128,512]{1,0:T(8,128)(2,1)}), bf16[4096,512]{1,0:T(8,128)(2,1)}) %all-gather.5.cloned.1.call-update) | async-done | bytes 4194320 | tf_op jit(solution)/shard_map/all_gather | solution.py:20
  403.6 7.7 %gather_fusion.3 = bf16[64,128,512]{2,1,0:T(8,128)(2,1)} fusion(bf16[32,128,512]{2,1,0:T(8,128)(2,1)} %bitcast.55, s32[1024]{0:T(1024)S(1)} %pad_clamp_fusion.2), kind=kCustom, calls=%fused_computation.1.clone | custom fusion | bytes 16777472 | tf_op jit(solution)/shard_map/jit(_take)/gather | solution.py:14
  411.3 5.7 %fusion = f32[16,128,512,1]{2,1,3,0:T(8,128)S(1)} fusion(bf16[16,4,128,512]{3,2,1,0:T(8,128)(2,1)} %bitcast.57, pred[16,4]{1,0:T(8,128)(4,1)S(1)} %copy.31, bf16[1,1,16,4,128,128]{5,4,3,2,1,0:T(8,128)(2,1)} %param.14, bf16[16,4]{1,0:T(8,128)(2,1)S(1)} %fusion.22), kind=kOutput, calls=%fused_computation.4 | convolution fusion | flops 1078984704 | bytes 14680256 | tf_op jit(solution)/shard_map/rkab,rkbf->raf/dot_general | solution.py:15
  417.0 1.9 copy-done.1
  419.3 5.9 %add.103 = f32[2048,512]{1,0:T(8,128)} dynamic-update-slice(f32[2048,512]{1,0:T(8,128)} %bitcast.60, f32[2048,32]{1,0:T(8,128)S(1)} %bitcast_add_fusion, s32[]{:T(128)} %constant.76.clone.1, s32[]{:T(128)S(6)} %select_n.66) | dynamic-update-slice | bytes 524292 | tf_op jit(solution)/shard_map/add | solution.py:23
  425.2 3.8 convert_element_type.47
  429.1 86.7 %reduce-scatter.5.cloned.1.call-done = bf16[128,512]{1,0:T(8,128)(2,1)} async-done(((bf16[2048,512]{1,0:T(8,128)(2,1)}), bf16[128,512]{1,0:T(8,128)(2,1)}) %reduce-scatter.5.cloned.1.call-update) | async-done | bytes 131088 | tf_op jit(solution)/shard_map/reduce_scatter | solution.py:25
  515.8 1.8 convolution_convert_fusion.1
  (43 shorter events, 2.6 us)
Async XLA Ops:
  7.2 302.6 %copy-start = (bf16[1,40,128,128]{3,2,1,0:T(8,128)(2,1)S(1)}, bf16[1,40,128,128]{3,2,1,0:T(8,128)(2,1)}, u32[]{:S(2)}) copy-start(bf16[1,40,128,128]{3,2,1,0:T(8,128)(2,1)} %param.19) | copy-start | bytes 3932164
  7.2 144.7 %all-gather.3.cloned.1.call-start = ((), (), s32[]{:S(2)}) async-start(), calls=%async_computation.3 | async-start | bytes 4325376 | tf_op jit(solution)/shard_map/all_gather | solution.py:20
  7.9 246.3 %reduce-scatter.3.cloned.1.call-start = ((), (), s32[]{:S(2)}) async-start(), calls=%async_computation.4 | async-start | bytes 2228224 | tf_op jit(solution)/shard_map/reduce_scatter | solution.py:25
  159.5 94.7 %copy-start.2 = (bf16[512,512]{1,0:T(8,128)(2,1)S(1)}, bf16[512,512]{1,0:T(8,128)(2,1)}, u32[]{:S(2)}) copy-start(bf16[512,512]{1,0:T(8,128)(2,1)} %param.22) | copy-start | bytes 1572868
  159.5 96.5 %copy-start.5 = (bf16[32,512]{1,0:T(8,128)(2,1)S(1)}, bf16[32,512]{1,0:T(8,128)(2,1)}, u32[]{:S(2)}) copy-start(bf16[32,512]{1,0:T(8,128)(2,1)} %param.17) | copy-start | bytes 98308
  159.5 96.6 %copy-start.4 = (s32[32,40]{1,0:T(8,128)S(1)}, s32[32,40]{1,0:T(8,128)}, u32[]{:S(2)}) copy-start(s32[32,40]{1,0:T(8,128)} %param.18) | copy-start | bytes 15364
  166.7 105.0 %copy-start.7 = (s32[1,40]{1,0:T(1,128)S(1)}, s32[1,40]{1,0:T(1,128)}, u32[]{:S(2)}) copy-start(s32[1,40]{1,0:T(1,128)} %param.21) | copy-start | bytes 484
  166.8 143.9 %copy-start.6 = (s32[1,40]{1,0:T(1,128)S(1)}, s32[1,40]{1,0:T(1,128)}, u32[]{:S(2)}) copy-start(s32[1,40]{1,0:T(1,128)} %param.20) | copy-start | bytes 484
  166.8 236.8 %all-gather.5.cloned.1.call-start = ((), (), s32[]{:S(2)}) async-start(), calls=%async_computation.5 | async-start | bytes 4325376 | tf_op jit(solution)/shard_map/all_gather | solution.py:20
  258.6 49.8 %all-to-all-start = ((bf16[32,2,32,128]{3,2,1,0:T(8,128)(2,1)}), bf16[32,2,32,128]{3,2,1,0:T(8,128)(2,1)S(1)}, u32[]{:S(2)}, u32[]{:S(2)}) async-start(bf16[32,2,32,128]{3,2,1,0:T(8,128)(2,1)} %copy.35), calls=%async_computation.1 | async-start | bytes 1048576 | tf_op jit(solution)/shard_map/all_to_all | solution.py:50
  271.7 244.1 %reduce-scatter.5.cloned.1.call-start = ((), (), s32[]{:S(2)}) async-start(), calls=%async_computation.6 | async-start | bytes 2228224 | tf_op jit(solution)/shard_map/reduce_scatter | solution.py:25
  417.0 2.0 copy-start.1
  425.2 90.6 %copy-start.3 = (bf16[512,512]{1,0:T(8,128)(2,1)S(1)}, bf16[512,512]{1,0:T(8,128)(2,1)}, u32[]{:S(2)}) copy-start(bf16[512,512]{1,0:T(8,128)(2,1)} %param.23) | copy-start | bytes 1572868
Sparse Core Ops, SparseCore 0:
  10.1 141.6 all-gather.2
  166.9 87.3 reduce-scatter.2
  257.1 146.4 all-gather.4
  429.2 86.5 reduce-scatter.4
where the time goes:
time: 525 us; the launch traced here: 524 us
  waiting for transfers between devices  445 us (85%)
  local copies, waits for them, and re-layouts  26.1 us (5%)
  matrix products  18.4 us (4%)
  between operations  14 us (3%)
  starting transfers between devices  13.2 us (3%)
  other arithmetic  7.57 us (1%)
    all_gather x2, waiting for transfers between devices, aggregate(): col_panel = lax.all_gather(source, 'dom', axis=0, tiled=True)  233 us
    reduce_scatter x2, waiting for transfers between devices, aggregate(): lax.psum_scatter(rounded.astype(jnp.float32).astype(jnp.bfloat16), 'grid'...  174 us
    all_to_all x1, waiting for transfers between devices, history_term(): lax.all_to_all(outgoing, 'dom', split_axis=0, concat_axis=0, tiled=True)  36.6 us
    gather x2, local copies, waits for them, and re-layouts, tile_product(): picked = jnp.take(blocks, tile_cols, axis=0)  15.4 us
    all_to_all x1, starting transfers between devices, history_term(): lax.all_to_all(outgoing, 'dom', split_axis=0, concat_axis=0, tiled=True)  13 us
    dot_general x2, matrix products, tile_product(): jnp.einsum('rkab,rkbf->raf', live_vals, picked, preferred_element_type=jn...  12.9 us
  transfers between devices with their start and end apart: 5, of which 5 were waited for; matrix products, arithmetic and copies ran while one was open for 2% of the time, Pallas kernels for 0%

commit v1 on v0

--- a/solution.py
+++ b/solution.py
@@ -17,7 +17,9 @@
 
 
 def aggregate(source, live_vals, tile_cols, extra_term):
-    col_panel = lax.all_gather(source, "dom", axis=0, tiled=True)
+    col_panel = jnp.concatenate(
+        lax.all_to_all(jnp.stack([source] * lax.axis_size("dom")), "dom", 0, 0), axis=0
+    )
     partial_value = tile_product(col_panel, live_vals, tile_cols)
     if extra_term is not None:
         partial_value = partial_value + extra_term

time: 525 us -> 643 us (1.22)
  the two profiles are of different devices: /device:TPU:32 before, /device:TPU:8 now
where the time goes in v1:
time: 643 us; the launch traced here: 642 us
  waiting for transfers between devices  533 us (83%)
  starting transfers between devices  38.7 us (6%)
  local copies, waits for them, and re-layouts  32.7 us (5%)
  matrix products  17.7 us (3%)
  between operations  14.3 us (2%)
    all_to_all x2, waiting for transfers between devices, aggregate(): lax.all_to_all(jnp.stack([source] * lax.axis_size('dom')), 'dom', 0, 0)  364 us
    reduce_scatter x2, waiting for transfers between devices, aggregate(): lax.psum_scatter(rounded.astype(jnp.float32).astype(jnp.bfloat16), 'grid'...  169 us
    all_to_all x2, starting transfers between devices, aggregate(): lax.all_to_all(jnp.stack([source] * lax.axis_size('dom')), 'dom', 0, 0)  29.6 us
    gather x2, local copies, waits for them, and re-layouts, tile_product(): picked = jnp.take(blocks, tile_cols, axis=0)  15.4 us
    dot_general x2, matrix products, tile_product(): jnp.einsum('rkab,rkbf->raf', live_vals, picked, preferred_element_type=jn...  12.9 us
  transfers between devices with their start and end apart: 5, of which 4 were waited for; matrix products, arithmetic and copies ran while one was open for 1% of the time, Pallas kernels for 0%

profile of v1, /device:TPU:8, one launch (start us, length us, event | category | flops | bytes accessed | tf_op | source)
XLA Modules:
  0.0 642.3 jit_solution(2572543220860690685)
XLA Ops:
  7.2 3.4 stack.4
  10.6 16.7 %all-to-all-start = ((bf16[32,128,512]{2,1,0:T(8,128)(2,1)}), bf16[32,128,512]{2,1,0:T(8,128)(2,1)}, u32[]{:S(2)}, u32[]{:S(2)}) async-start(bf16[32,128,512]{2,1,0:T(8,128)(2,1)} %stack.4), calls=%async_computation | async-start | bytes 8388608 | tf_op jit(solution)/shard_map/all_to_all | solution.py:21
  27.8 184.2 %all-to-all-done = bf16[32,128,512]{2,1,0:T(8,128)(2,1)} async-done(((bf16[32,128,512]{2,1,0:T(8,128)(2,1)}), bf16[32,128,512]{2,1,0:T(8,128)(2,1)}, u32[]{:S(2)}, u32[]{:S(2)}) %all-to-all-start) | async-done | bytes 4194336 | tf_op jit(solution)/shard_map/all_to_all | solution.py:21
  212.0 7.7 %gather_fusion.2 = bf16[64,128,512]{2,1,0:T(8,128)(2,1)} fusion(bf16[32,128,512]{2,1,0:T(8,128)(2,1)} %all-to-all-done, s32[1024]{0:T(1024)S(1)} %pad_clamp_fusion.2), kind=kCustom, calls=%fused_computation.clone | custom fusion | bytes 16777472 | tf_op jit(solution)/shard_map/jit(_take)/gather | solution.py:14
  219.7 7.2 %bitcast_convert_fusion = bf16[16,128,512]{2,1,0:T(8,128)(2,1)} fusion(bf16[16,4,128,512]{3,2,1,0:T(8,128)(2,1)} %bitcast.54, pred[16,4]{1,0:T(8,128)(4,1)S(1)} %copy.31, bf16[1,1,16,4,128,128]{5,4,3,2,1,0:T(8,128)(2,1)} %param.14, bf16[16,4]{1,0:T(8,128)(2,1)S(1)} %fusion.22), kind=kOutput, calls=%fused_computation.10 | convolution fusion | flops 1080033280 | bytes 12583104 | tf_op jit(solution)/shard_map/rkab,rkbf->raf/dot_general | solution.py:15
  226.9 0.8 convert_reduce_fusion
  228.4 1.0 copy.35
  229.4 9.0 %all-to-all-start.2 = ((bf16[32,2,32,128]{3,2,1,0:T(8,128)(2,1)}), bf16[32,2,32,128]{3,2,1,0:T(8,128)(2,1)S(1)}, u32[]{:S(2)}, u32[]{:S(2)}) async-start(bf16[32,2,32,128]{3,2,1,0:T(8,128)(2,1)} %copy.35), calls=%async_computation.3 | async-start | bytes 1048576 | tf_op jit(solution)/shard_map/all_to_all | solution.py:52
  238.4 80.0 %reduce-scatter.3.cloned.1.call-done = bf16[128,512]{1,0:T(8,128)(2,1)} async-done(((bf16[2048,512]{1,0:T(8,128)(2,1)}), bf16[128,512]{1,0:T(8,128)(2,1)}) %reduce-scatter.3.cloned.1.call-update) | async-done | bytes 131088 | tf_op jit(solution)/shard_map/reduce_scatter | solution.py:27
  318.4 1.1 fusion.12
  319.6 2.4 stack.5
  322.0 13.0 %all-to-all-start.1 = ((bf16[32,128,512]{2,1,0:T(8,128)(2,1)}), bf16[32,128,512]{2,1,0:T(8,128)(2,1)}, u32[]{:S(2)}, u32[]{:S(2)}) async-start(bf16[32,128,512]{2,1,0:T(8,128)(2,1)} %stack.5), calls=%async_computation.2 | async-start | bytes 8388608 | tf_op jit(solution)/shard_map/all_to_all | solution.py:21
  335.1 0.6 gather_fusion
  335.9 0.6 gather_fusion.1
  336.5 0.8 fusion.10
  337.3 0.7 convolution_bitcast_fusion
  338.4 180.1 %all-to-all-done.1 = bf16[32,128,512]{2,1,0:T(8,128)(2,1)} async-done(((bf16[32,128,512]{2,1,0:T(8,128)(2,1)}), bf16[32,128,512]{2,1,0:T(8,128)(2,1)}, u32[]{:S(2)}, u32[]{:S(2)}) %all-to-all-start.1) | async-done | bytes 4194336 | tf_op jit(solution)/shard_map/all_to_all | solution.py:21
  518.5 7.7 %gather_fusion.3 = bf16[64,128,512]{2,1,0:T(8,128)(2,1)} fusion(bf16[32,128,512]{2,1,0:T(8,128)(2,1)} %all-to-all-done.1, s32[1024]{0:T(1024)S(1)} %pad_clamp_fusion.2), kind=kCustom, calls=%fused_computation.1.clone | custom fusion | bytes 16777472 | tf_op jit(solution)/shard_map/jit(_take)/gather | solution.py:14
  526.2 5.7 fusion
  531.9 1.9 copy-done.1
  534.3 6.6 %add.103 = f32[2048,512]{1,0:T(8,128)} dynamic-update-slice(f32[2048,512]{1,0:T(8,128)} %bitcast.56, f32[2048,32]{1,0:T(8,128)S(1)} %bitcast_add_fusion, s32[]{:T(128)} %constant.76.clone.1, s32[]{:T(128)S(6)} %select_n.66) | dynamic-update-slice | bytes 524292 | tf_op jit(solution)/shard_map/add | solution.py:25
  540.9 3.9 convert_element_type.47
  544.7 89.0 %reduce-scatter.5.cloned.1.call-done = bf16[128,512]{1,0:T(8,128)(2,1)} async-done(((bf16[2048,512]{1,0:T(8,128)(2,1)}), bf16[128,512]{1,0:T(8,128)(2,1)}) %reduce-scatter.5.cloned.1.call-update) | async-done | bytes 131088 | tf_op jit(solution)/shard_map/reduce_scatter | solution.py:27
  633.7 1.8 convolution_convert_fusion.1
  (49 shorter events, 2.0 us)
Async XLA Ops:
  7.2 329.3 %copy-start = (bf16[1,40,128,128]{3,2,1,0:T(8,128)(2,1)S(1)}, bf16[1,40,128,128]{3,2,1,0:T(8,128)(2,1)}, u32[]{:S(2)}) copy-start(bf16[1,40,128,128]{3,2,1,0:T(8,128)(2,1)} %param.19) | copy-start | bytes 3932164
  10.6 16.7 %copy-start.7 = (s32[1,1,16,4]{2,3,1,0:T(4,128)S(1)}, s32[1,1,16,4]{2,3,1,0:T(4,128)}, u32[]{:S(2)}) copy-start(s32[1,1,16,4]{2,3,1,0:T(4,128)} %param.15) | copy-start | bytes 772
  10.6 17.0 %copy-start.6 = (bf16[32,512]{1,0:T(8,128)(2,1)S(1)}, bf16[32,512]{1,0:T(8,128)(2,1)}, u32[]{:S(2)}) copy-start(bf16[32,512]{1,0:T(8,128)(2,1)} %param.17) | copy-start | bytes 98308
  10.6 17.1 %copy-start.9 = (s32[1,1,16]{2,1,0:T(1,128)S(1)}, s32[1,1,16]{2,1,0:T(1,128)}, u32[]{:S(2)}) copy-start(s32[1,1,16]{2,1,0:T(1,128)} %param.16) | copy-start | bytes 196
  10.6 201.3 %all-to-all-start = ((bf16[32,128,512]{2,1,0:T(8,128)(2,1)}), bf16[32,128,512]{2,1,0:T(8,128)(2,1)}, u32[]{:S(2)}, u32[]{:S(2)}) async-start(bf16[32,128,512]{2,1,0:T(8,128)(2,1)} %stack.4), calls=%async_computation | async-start | bytes 8388608 | tf_op jit(solution)/shard_map/all_to_all | solution.py:21
  27.3 291.2 %reduce-scatter.3.cloned.1.call-start = ((), (), s32[]{:S(2)}) async-start(), calls=%async_computation.5 | async-start | bytes 2228224 | tf_op jit(solution)/shard_map/reduce_scatter | solution.py:27
  219.7 7.2 %copy-start.5 = (s32[32,40]{1,0:T(8,128)S(1)}, s32[32,40]{1,0:T(8,128)}, u32[]{:S(2)}) copy-start(s32[32,40]{1,0:T(8,128)} %param.18) | copy-start | bytes 15364
  226.9 91.6 %copy-start.2 = (bf16[512,512]{1,0:T(8,128)(2,1)S(1)}, bf16[512,512]{1,0:T(8,128)(2,1)}, u32[]{:S(2)}) copy-start(bf16[512,512]{1,0:T(8,128)(2,1)} %param.22) | copy-start | bytes 1572868
  229.4 90.2 %all-to-all-start.2 = ((bf16[32,2,32,128]{3,2,1,0:T(8,128)(2,1)}), bf16[32,2,32,128]{3,2,1,0:T(8,128)(2,1)S(1)}, u32[]{:S(2)}, u32[]{:S(2)}) async-start(bf16[32,2,32,128]{3,2,1,0:T(8,128)(2,1)} %copy.35), calls=%async_computation.3 | async-start | bytes 1048576 | tf_op jit(solution)/shard_map/all_to_all | solution.py:52
  319.6 2.4 copy-start.4
  322.0 13.1 %copy-start.10 = (s32[1,40]{1,0:T(1,128)S(1)}, s32[1,40]{1,0:T(1,128)}, u32[]{:S(2)}) copy-start(s32[1,40]{1,0:T(1,128)} %param.21) | copy-start | bytes 484
  322.0 196.5 %all-to-all-start.1 = ((bf16[32,128,512]{2,1,0:T(8,128)(2,1)}), bf16[32,128,512]{2,1,0:T(8,128)(2,1)}, u32[]{:S(2)}, u32[]{:S(2)}) async-start(bf16[32,128,512]{2,1,0:T(8,128)(2,1)} %stack.5), calls=%async_computation.2 | async-start | bytes 8388608 | tf_op jit(solution)/shard_map/all_to_all | solution.py:21
  335.0 2.3 copy-start.8
  335.0 298.7 %reduce-scatter.5.cloned.1.call-start = ((), (), s32[]{:S(2)}) async-start(), calls=%async_computation.6 | async-start | bytes 2228224 | tf_op jit(solution)/shard_map/reduce_scatter | solution.py:27
  531.9 1.9 copy-start.1
  540.9 92.8 %copy-start.3 = (bf16[512,512]{1,0:T(8,128)(2,1)S(1)}, bf16[512,512]{1,0:T(8,128)(2,1)}, u32[]{:S(2)}) copy-start(bf16[512,512]{1,0:T(8,128)(2,1)} %param.23) | copy-start | bytes 1572868
Sparse Core Ops, SparseCore 0:
  227.0 91.3 reduce-scatter.2
  544.9 88.7 reduce-scatter.4
